TPU v7x, 32 devices: a whole 2x2x4 slice. The times are simulated.
32 devices in a mesh: dp: 8 (over y, x, core), ctx: 4 (over z).
Axes of the slice: x: 2, y: 2, z: 4, core: 2. Of those that a mesh axis runs over, the one named last changes fastest.
Arguments:
- queries: bfloat16 [8192, 2048], P(('dp', 'ctx')), parts along dimension 0, may hold values from -18 to 18
- key_vectors: bfloat16 [8192, 2048], P(('dp', 'ctx')), parts along dimension 0, may hold values from -18 to 18
- value_vectors: bfloat16 [8192, 2048], P(('dp', 'ctx')), parts along dimension 0, may hold values from -6 to 6
- norm_gain: float32 [2048], replicated, may hold values from 0.1 to 1.9
- window_gain: float32 [2048], replicated, may hold values from 0.1 to 1.9
Outputs:
- mixed: bfloat16 [8192, 2048], P(('dp', 'ctx')), parts along dimension 0
There are 8 independent parts, one for each index of `dp`. A program takes and returns all parts, laid end to end along the dimension named above; an argument that names none is the same for every part. Nothing has to cross between parts.
All inputs are finite; a program needn't handle non-finite values.
Results may differ from a plain program's by a relative error of at most 0.0037.
Values may be sent and summed in bfloat16 or wider, within the bound.
A program may use at most 128 MiB of HBM per device.

v0:
```python
import math

import jax
import jax.numpy as jnp
from jax import lax
from jax.sharding import PartitionSpec as P

HEAD = 128
WINDOW = 1024


def passed_along(value, axis, steps):
    count = lax.axis_size(axis)
    leading, last = (max(0, -steps), min(count, count - steps))
    return lax.ppermute(value, axis, [(source, source + steps) for source in range(leading, last)])


def entering(array, axis, combine, identity):
    peers, position = (lax.axis_size(axis), lax.axis_index(axis))
    everything = lax.all_gather(array.astype(jnp.bfloat16), axis)
    start = jnp.broadcast_to(jnp.asarray(identity, array.dtype), array.shape)

    def lap(k, before):
        reached = k < position
        new = combine(before, everything[k].astype(array.dtype))
        return jnp.where(reached, new, before)

    return lax.fori_loop(0, peers, lap, start)


def feature_map(values):
    upcast = values.astype(jnp.float32)
    return jnp.where(upcast > 0, upcast + 1.0, jnp.exp(jnp.minimum(upcast, 0.0))).astype(
        jnp.bfloat16
    )


def add_states(earlier, later):
    return earlier + later


def shards(queries, key_vectors, value_vectors, norm_gain, window_gain):
    tok_rows, model_width = queries.shape
    head_count = model_width // HEAD
    ctx_index = lax.axis_index("ctx")
    reach_blocks = WINDOW // tok_rows
    own_pair = (key_vectors, value_vectors)
    received = []
    travelling = own_pair
    for distance in range(reach_blocks):
        travelling = passed_along((travelling[0], travelling[1]), "ctx", 1)
        received.append(travelling)
    ordered = received[::-1] + [own_pair]
    window_keys = jnp.concatenate([member[0] for member in ordered], axis=0)
    window_values = jnp.concatenate([member[1] for member in ordered], axis=0)
    span_rows = window_keys.shape[0]
    query_place = ctx_index * tok_rows + jnp.arange(tok_rows, dtype=jnp.int32)
    key_place = (ctx_index - reach_blocks) * tok_rows + jnp.arange(span_rows, dtype=jnp.int32)
    inside = (
        (key_place[None, :] <= query_place[:, None])
        & (query_place[:, None] - key_place[None, :] < WINDOW)
        & (key_place[None, :] >= 0)
    )
    group_size = 4
    groups = head_count // group_size
    scale = 1.0 / math.sqrt(HEAD)

    def split_groups(matrix):
        return jnp.moveaxis(matrix.reshape(matrix.shape[0], groups, group_size, HEAD), 1, 0)

    def attend(operands):
        query_group, key_group, value_group = operands
        scores = (
            jnp.einsum("tge,sge->gts", query_group, key_group, preferred_element_type=jnp.float32)
            * scale
        )
        scores = jnp.where(inside[None], scores, -jnp.inf)
        peak = jnp.max(scores, axis=-1, keepdims=True)
        expos = jnp.exp(scores - peak)
        weights = (expos / jnp.sum(expos, axis=-1, keepdims=True)).astype(jnp.bfloat16)
        return jnp.einsum("gts,sge->tge", weights, value_group, preferred_element_type=jnp.float32)

    attended = lax.map(
        attend, (split_groups(queries), split_groups(window_keys), split_groups(window_values))
    )
    attended = jnp.moveaxis(attended, 0, 1).reshape(tok_rows, head_count, HEAD)
    windowed = attended * lax.rsqrt(jnp.mean(attended * attended, axis=-1, keepdims=True) + 1e-05)
    windowed = windowed * window_gain.reshape(head_count, HEAD)
    phi_query = feature_map(queries).reshape(tok_rows, head_count, HEAD)
    phi_key = feature_map(key_vectors).reshape(tok_rows, head_count, HEAD)
    value_heads = value_vectors.reshape(tok_rows, head_count, HEAD)
    local_state = jnp.einsum(
        "the,thf->hef", phi_key, value_heads, preferred_element_type=jnp.float32
    )
    carried = entering(local_state, "ctx", add_states, jnp.zeros_like(local_state))
    from_state = jnp.einsum(
        "the,hef->thf", phi_query, carried.astype(jnp.bfloat16), preferred_element_type=jnp.float32
    )
    affinity = jnp.einsum("the,she->hts", phi_query, phi_key, preferred_element_type=jnp.float32)
    inner = jnp.arange(tok_rows, dtype=jnp.int32)
    causal = inner[:, None] >= inner[None, :]
    affinity = jnp.where(causal[None], affinity, 0.0).astype(jnp.bfloat16)
    local_part = jnp.einsum(
        "hts,shf->thf", affinity, value_heads, preferred_element_type=jnp.float32
    )
    linear = from_state + local_part
    normed = linear * lax.rsqrt(jnp.mean(linear * linear, axis=-1, keepdims=True) + 1e-05)
    normed = normed * norm_gain.reshape(head_count, HEAD)
    return (windowed + normed).reshape(tok_rows, model_width).astype(jnp.bfloat16)


def solution(mesh):
    return jax.shard_map(
        shards,
        mesh=mesh,
        in_specs=(P(("dp", "ctx"), None), P(("dp", "ctx"), None), P(("dp", "ctx"), None), P(), P()),
        out_specs=P(("dp", "ctx"), None),
        check_vma=False,
    )
```

profile of v0, /device:TPU:30, one launch (start us, length us, event | category | flops | bytes accessed | tf_op | source)
XLA Modules:
  0.0 289.3 jit_solution(14858357100028884899)
XLA Ops:
  12.1 2.8 convolution_convert_fusion
  14.9 39.0 %collective-permute-done.4 = bf16[256,2048]{0,1:T(8,128)(2,1)} collective-permute-done((bf16[256,2048]{0,1:T(8,128)(2,1)S(1)}, bf16[256,2048]{0,1:T(8,128)(2,1)}, u32[]{:S(2)}, u32[]{:S(2)}) %collective-permute-start.4) | collective-permute-done | bytes 1048608 | tf_op jit(solution)/shard_map/ppermute | solution.py:15
  55.2 37.2 %collective-permute-done = bf16[256,2048]{1,0:T(8,128)(2,1)} collective-permute-done((bf16[256,2048]{1,0:T(8,128)(2,1)S(1)}, bf16[256,2048]{1,0:T(8,128)(2,1)}, u32[]{:S(2)}, u32[]{:S(2)}) %collective-permute-start) | collective-permute-done | bytes 1048608 | tf_op jit(solution)/shard_map/ppermute | solution.py:15
  93.7 21.1 %collective-permute-done.5 = bf16[256,2048]{0,1:T(8,128)(2,1)S(1)} collective-permute-done((bf16[256,2048]{0,1:T(8,128)(2,1)}, bf16[256,2048]{0,1:T(8,128)(2,1)S(1)}, u32[]{:S(2)}, u32[]{:S(2)}) %collective-permute-start.5) | collective-permute-done | bytes 1048608 | tf_op jit(solution)/shard_map/ppermute | solution.py:15
  116.0 21.2 %collective-permute-done.1 = bf16[256,2048]{1,0:T(8,128)(2,1)S(1)} collective-permute-done((bf16[256,2048]{1,0:T(8,128)(2,1)}, bf16[256,2048]{1,0:T(8,128)(2,1)S(1)}, u32[]{:S(2)}, u32[]{:S(2)}) %collective-permute-start.1) | collective-permute-done | bytes 1048608 | tf_op jit(solution)/shard_map/ppermute | solution.py:15
  140.9 5.0 %fusion.63 = f32[16,256,128]{1,2,0:T(8,128)} fusion(bf16[256,16,128]{0,2,1:T(8,128)(2,1)} %bitcast.127, pred[256,256]{1,0:T(8,128)(4,1)S(1)} %iota_compare_fusion, bf16[256,2048]{1,0:T(8,128)(2,1)} %param.10, bf16[256,2048]{1,0:T(8,128)(2,1)} %param.9), kind=kOutput, calls=%fused_computation.51 | convolution fusion | flops 545259520 | bytes 5308416 | tf_op jit(solution)/shard_map/hts,shf->thf/dot_general | solution.py:103
  145.9 13.9 %collective-permute-done.6 = bf16[256,2048]{0,1:T(8,128)(2,1)} collective-permute-done((bf16[256,2048]{0,1:T(8,128)(2,1)S(1)}, bf16[256,2048]{0,1:T(8,128)(2,1)}, u32[]{:S(2)}, u32[]{:S(2)}) %collective-permute-start.6) | collective-permute-done | bytes 1048608 | tf_op jit(solution)/shard_map/ppermute | solution.py:15
  161.1 21.2 %collective-permute-done.2 = bf16[256,2048]{1,0:T(8,128)(2,1)} collective-permute-done((bf16[256,2048]{1,0:T(8,128)(2,1)S(1)}, bf16[256,2048]{1,0:T(8,128)(2,1)}, u32[]{:S(2)}, u32[]{:S(2)}) %collective-permute-start.2) | collective-permute-done | bytes 1048608 | tf_op jit(solution)/shard_map/ppermute | solution.py:15
  183.8 6.6 %while.26 = (s32[]{:T(128)}, f32[16,128,128]{2,1,0:T(8,128)S(1)}, s32[]{:T(128)}, bf16[4,16,128,128]{3,2,1,0:T(8,128)(2,1)}, s32[]{:T(128)}, /*index=5*/s32[]{:T(128)}) while((s32[]{:T(128)}, f32[16,128,128]{2,1,0:T(8,128)S(1)}, s32[]{:T(128)}, bf16[4,16,128,128]{3,2,1,0:T(8,128)(2,1)}, s32[]{:T(128)}, /*index=5*/s32[]{:T(128)}) %tuple.60), condition=%wide.region_6.7_spmd.clone, body=%wide.region_5.6_spmd.clone.sunk | while | flops 1048580 | bytes 2621533 | solution.py:28
  190.3 2.8 multiply_reduce_fusion
  193.1 11.6 %collective-permute-done.7 = bf16[256,2048]{0,1:T(8,128)(2,1)} collective-permute-done((bf16[256,2048]{0,1:T(8,128)(2,1)}, bf16[256,2048]{0,1:T(8,128)(2,1)}, u32[]{:S(2)}, u32[]{:S(2)}) %collective-permute-start.7) | collective-permute-done | bytes 1048608 | tf_op jit(solution)/shard_map/ppermute | solution.py:15
  209.0 17.1 %collective-permute-done.3 = bf16[256,2048]{1,0:T(8,128)(2,1)} collective-permute-done((bf16[256,2048]{1,0:T(8,128)(2,1)}, bf16[256,2048]{1,0:T(8,128)(2,1)}, u32[]{:S(2)}, u32[]{:S(2)}) %collective-permute-start.3) | collective-permute-done | bytes 1048608 | tf_op jit(solution)/shard_map/ppermute | solution.py:15
  226.1 2.3 constant_dynamic-update-slice_fusion.4
  228.4 2.3 constant_dynamic-update-slice_fusion.3
  235.2 8.0 %copy.25 = bf16[1280,2048]{0,1:T(8,128)(2,1)} copy(bf16[1280,2048]{1,0:T(8,128)(2,1)} %constant_dynamic-update-slice_fusion) | data formatting | bytes 10485760 | tf_op jit(solution)/shard_map/concatenate | solution.py:55
  243.2 34.0 %while.25 = (s32[]{:T(128)}, f32[4,256,4,128]{1,3,2,0:T(8,128)}, bf16[4,1280,4,128]{1,3,2,0:T(8,128)(2,1)}, bf16[4,256,4,128]{1,3,2,0:T(8,128)(2,1)S(1)}, bf16[4...) while((s32[]{:T(128)}, f32[4,256,4,128]{1,3,2,0:T(8,128)}, ...), condition=%wide.region_3.4_spmd.clone, body=%wide.region_0.3_spmd.clone.sunk | while | flops 1020071424 | bytes 5982557 | solution.py:83
  243.6 3.3 %exponential_reduce_fusion.2 = f32[4,256]{1,0:T(4,128)S(1)} fusion(pred[256,1280]{1,0:T(8,128)(4,1)S(1)} %fusion.108, bf16[4,1280,4,128]{1,3,2,0:T(8,128)(2,1)} %get-tuple-element.292, s32[]{:T(128)} %get-tuple-element.279, bf16[4,256,4,128]{1,3,2,0:T(8,128)(2,1)S(1)} %get-tuple-element.291), kind=kOutput, calls=%fused_computation.5.clone.1 | convolution fusion | flops 340788480 | bytes 1905664 | tf_op jit(solution)/shard_map/while/body/eval_jaxpr/sub | solution.py:79
  246.9 4.8 %fusion.109 = f32[4,256,4,128]{1,3,2,0:T(8,128)} fusion(f32[4,256,4,128]{1,3,2,0:T(8,128)} %get-tuple-element.280, s32[]{:T(128)} %get-tuple-element.279, f32[4,256]{1,0:T(4,128)S(1)} %exponential_reduce_fusion.2, bf16[4,1280,4,128]{1,3,2,0:T(8,128)(2,1)} %get-tuple-element.290, pred[256,1280]{1,0:T(8,128)(4,1)S(1)} %fusion.108, ...), kind=kOutput, calls=%fused_computation.15.clone.1 | convolution fusion | flops 677644544 | bytes 3741696 | tf_op jit(solution)/shard_map/while/body/eval_jaxpr/gts,sge->tge/dot_general | solution.py:81
  252.1 3.3 %exponential_reduce_fusion.2 = f32[4,256]{1,0:T(4,128)S(1)} fusion(pred[256,1280]{1,0:T(8,128)(4,1)S(1)} %fusion.108, bf16[4,1280,4,128]{1,3,2,0:T(8,128)(2,1)} %get-tuple-element.292, s32[]{:T(128)} %get-tuple-element.279, bf16[4,256,4,128]{1,3,2,0:T(8,128)(2,1)S(1)} %get-tuple-element.291), kind=kOutput, calls=%fused_computation.5.clone.1 | convolution fusion | flops 340788480 | bytes 1905664 | tf_op jit(solution)/shard_map/while/body/eval_jaxpr/sub | solution.py:79
  255.4 4.8 %fusion.109 = f32[4,256,4,128]{1,3,2,0:T(8,128)} fusion(f32[4,256,4,128]{1,3,2,0:T(8,128)} %get-tuple-element.280, s32[]{:T(128)} %get-tuple-element.279, f32[4,256]{1,0:T(4,128)S(1)} %exponential_reduce_fusion.2, bf16[4,1280,4,128]{1,3,2,0:T(8,128)(2,1)} %get-tuple-element.290, pred[256,1280]{1,0:T(8,128)(4,1)S(1)} %fusion.108, ...), kind=kOutput, calls=%fused_computation.15.clone.1 | convolution fusion | flops 677644544 | bytes 3741696 | tf_op jit(solution)/shard_map/while/body/eval_jaxpr/gts,sge->tge/dot_general | solution.py:81
  260.6 3.3 %exponential_reduce_fusion.2 = f32[4,256]{1,0:T(4,128)S(1)} fusion(pred[256,1280]{1,0:T(8,128)(4,1)S(1)} %fusion.108, bf16[4,1280,4,128]{1,3,2,0:T(8,128)(2,1)} %get-tuple-element.292, s32[]{:T(128)} %get-tuple-element.279, bf16[4,256,4,128]{1,3,2,0:T(8,128)(2,1)S(1)} %get-tuple-element.291), kind=kOutput, calls=%fused_computation.5.clone.1 | convolution fusion | flops 340788480 | bytes 1905664 | tf_op jit(solution)/shard_map/while/body/eval_jaxpr/sub | solution.py:79
  263.9 4.8 %fusion.109 = f32[4,256,4,128]{1,3,2,0:T(8,128)} fusion(f32[4,256,4,128]{1,3,2,0:T(8,128)} %get-tuple-element.280, s32[]{:T(128)} %get-tuple-element.279, f32[4,256]{1,0:T(4,128)S(1)} %exponential_reduce_fusion.2, bf16[4,1280,4,128]{1,3,2,0:T(8,128)(2,1)} %get-tuple-element.290, pred[256,1280]{1,0:T(8,128)(4,1)S(1)} %fusion.108, ...), kind=kOutput, calls=%fused_computation.15.clone.1 | convolution fusion | flops 677644544 | bytes 3741696 | tf_op jit(solution)/shard_map/while/body/eval_jaxpr/gts,sge->tge/dot_general | solution.py:81
  269.1 3.3 %exponential_reduce_fusion.2 = f32[4,256]{1,0:T(4,128)S(1)} fusion(pred[256,1280]{1,0:T(8,128)(4,1)S(1)} %fusion.108, bf16[4,1280,4,128]{1,3,2,0:T(8,128)(2,1)} %get-tuple-element.292, s32[]{:T(128)} %get-tuple-element.279, bf16[4,256,4,128]{1,3,2,0:T(8,128)(2,1)S(1)} %get-tuple-element.291), kind=kOutput, calls=%fused_computation.5.clone.1 | convolution fusion | flops 340788480 | bytes 1905664 | tf_op jit(solution)/shard_map/while/body/eval_jaxpr/sub | solution.py:79
  272.4 4.8 %fusion.109 = f32[4,256,4,128]{1,3,2,0:T(8,128)} fusion(f32[4,256,4,128]{1,3,2,0:T(8,128)} %get-tuple-element.280, s32[]{:T(128)} %get-tuple-element.279, f32[4,256]{1,0:T(4,128)S(1)} %exponential_reduce_fusion.2, bf16[4,1280,4,128]{1,3,2,0:T(8,128)(2,1)} %get-tuple-element.290, pred[256,1280]{1,0:T(8,128)(4,1)S(1)} %fusion.108, ...), kind=kOutput, calls=%fused_computation.15.clone.1 | convolution fusion | flops 677644544 | bytes 3741696 | tf_op jit(solution)/shard_map/while/body/eval_jaxpr/gts,sge->tge/dot_general | solution.py:81
  (68 shorter events, 37.8 us)
Async XLA Ops:
  6.5 5.6 %copy-start.4 = (bf16[256,2048]{1,0:T(8,128)(2,1)S(1)}, bf16[256,2048]{1,0:T(8,128)(2,1)}, u32[]{:S(2)}) copy-start(bf16[256,2048]{1,0:T(8,128)(2,1)} %param.10) | copy-start | bytes 3145732
  6.5 2.9 %copy-start = (bf16[256,2048]{1,0:T(8,128)(2,1)S(1)}, bf16[256,2048]{1,0:T(8,128)(2,1)}, u32[]{:S(2)}) copy-start(bf16[256,2048]{1,0:T(8,128)(2,1)} %param.11) | copy-start | bytes 3145732
  6.5 177.2 %all-gather.3.cloned.1.call-start = ((), (), s32[]{:S(2)}) async-start(), calls=%async_computation | async-start | bytes 2621440 | tf_op jit(solution)/shard_map/all_gather | solution.py:20
  8.2 6.7 %copy-start.2 = (bf16[256,2048]{0,1:T(8,128)(2,1)}, bf16[256,2048]{0,1:T(8,128)(2,1)S(1)}, u32[]{:S(2)}) copy-start(bf16[256,2048]{0,1:T(8,128)(2,1)S(1)} %copy.27) | copy-start | bytes 3145732
  8.2 45.8 %collective-permute-start.4 = (bf16[256,2048]{0,1:T(8,128)(2,1)S(1)}, bf16[256,2048]{0,1:T(8,128)(2,1)}, u32[]{:S(2)}, u32[]{:S(2)}) collective-permute-start(bf16[256,2048]{0,1:T(8,128)(2,1)S(1)} %copy.27), channel_id=1, source_target_pairs={{0,1},{1,2},{2,3},{4,5},{5,6},{6,7},{8,9},{9,10},{10,11},{12,13},{... | collective-permute-start | bytes 3145736 | tf_op jit(solution)/shard_map/ppermute | solution.py:15
  9.5 82.9 %collective-permute-start = (bf16[256,2048]{1,0:T(8,128)(2,1)S(1)}, bf16[256,2048]{1,0:T(8,128)(2,1)}, u32[]{:S(2)}, u32[]{:S(2)}) collective-permute-start(bf16[256,2048]{1,0:T(8,128)(2,1)S(1)} %copy-done), channel_id=1, source_target_pairs={{0,1},{1,2},{2,3},{4,5},{5,6},{6,7},{8,9},{9,10},{10,11},{12,13},{... | collective-permute-start | bytes 3145736 | tf_op jit(solution)/shard_map/ppermute | solution.py:15
  53.9 60.8 %collective-permute-start.5 = (bf16[256,2048]{0,1:T(8,128)(2,1)}, bf16[256,2048]{0,1:T(8,128)(2,1)S(1)}, u32[]{:S(2)}, u32[]{:S(2)}) collective-permute-start(bf16[256,2048]{0,1:T(8,128)(2,1)} %collective-permute-done.4), channel_id=1, source_target_pairs={{0,1},{1,2},{2,3},{4,5},{5,6},{6,7},{8,9},{9,10},{10,11},{12,13},{... | collective-permute-start | bytes 3145736 | tf_op jit(solution)/shard_map/ppermute | solution.py:15
  92.4 44.8 %collective-permute-start.1 = (bf16[256,2048]{1,0:T(8,128)(2,1)}, bf16[256,2048]{1,0:T(8,128)(2,1)S(1)}, u32[]{:S(2)}, u32[]{:S(2)}) collective-permute-start(bf16[256,2048]{1,0:T(8,128)(2,1)} %collective-permute-done), channel_id=1, source_target_pairs={{0,1},{1,2},{2,3},{4,5},{5,6},{6,7},{8,9},{9,10},{10,11},{12,13},{... | collective-permute-start | bytes 3145736 | tf_op jit(solution)/shard_map/ppermute | solution.py:15
  114.8 31.1 %copy-start.8 = (bf16[256,2048]{0,1:T(8,128)(2,1)}, bf16[256,2048]{0,1:T(8,128)(2,1)S(1)}, u32[]{:S(2)}) copy-start(bf16[256,2048]{0,1:T(8,128)(2,1)S(1)} %collective-permute-done.5) | copy-start | bytes 3145732
  114.8 45.0 %collective-permute-start.6 = (bf16[256,2048]{0,1:T(8,128)(2,1)S(1)}, bf16[256,2048]{0,1:T(8,128)(2,1)}, u32[]{:S(2)}, u32[]{:S(2)}) collective-permute-start(bf16[256,2048]{0,1:T(8,128)(2,1)S(1)} %collective-permute-done.5), channel_id=1, source_target_pairs={{0,1},{1,2},{2,3},{4,5},{5,6},{6,7},{8,9},{9,10},{10,11},{12,13},{... | collective-permute-start | bytes 3145736 | tf_op jit(solution)/shard_map/ppermute | solution.py:15
  137.2 8.6 %copy-start.6 = (bf16[256,2048]{1,0:T(8,128)(2,1)}, bf16[256,2048]{1,0:T(8,128)(2,1)S(1)}, u32[]{:S(2)}) copy-start(bf16[256,2048]{1,0:T(8,128)(2,1)S(1)} %collective-permute-done.1) | copy-start | bytes 3145732
  137.2 45.0 %collective-permute-start.2 = (bf16[256,2048]{1,0:T(8,128)(2,1)S(1)}, bf16[256,2048]{1,0:T(8,128)(2,1)}, u32[]{:S(2)}, u32[]{:S(2)}) collective-permute-start(bf16[256,2048]{1,0:T(8,128)(2,1)S(1)} %collective-permute-done.1), channel_id=1, source_target_pairs={{0,1},{1,2},{2,3},{4,5},{5,6},{6,7},{8,9},{9,10},{10,11},{12,13},{... | collective-permute-start | bytes 3145736 | tf_op jit(solution)/shard_map/ppermute | solution.py:15
  159.8 44.9 %collective-permute-start.7 = (bf16[256,2048]{0,1:T(8,128)(2,1)}, bf16[256,2048]{0,1:T(8,128)(2,1)}, u32[]{:S(2)}, u32[]{:S(2)}) collective-permute-start(bf16[256,2048]{0,1:T(8,128)(2,1)} %collective-permute-done.6), channel_id=1, source_target_pairs={{0,1},{1,2},{2,3},{4,5},{5,6},{6,7},{8,9},{9,10},{10,11},{12,13},{... | collective-permute-start | bytes 3145736 | tf_op jit(solution)/shard_map/ppermute | solution.py:15
  182.3 43.8 %collective-permute-start.3 = (bf16[256,2048]{1,0:T(8,128)(2,1)}, bf16[256,2048]{1,0:T(8,128)(2,1)}, u32[]{:S(2)}, u32[]{:S(2)}) collective-permute-start(bf16[256,2048]{1,0:T(8,128)(2,1)} %collective-permute-done.2), channel_id=1, source_target_pairs={{0,1},{1,2},{2,3},{4,5},{5,6},{6,7},{8,9},{9,10},{10,11},{12,13},{... | collective-permute-start | bytes 3145736 | tf_op jit(solution)/shard_map/ppermute | solution.py:15
  193.1 14.2 %copy-start.9 = (bf16[256,2048]{0,1:T(8,128)(2,1)S(1)}, bf16[256,2048]{0,1:T(8,128)(2,1)}, u32[]{:S(2)}) copy-start(bf16[256,2048]{0,1:T(8,128)(2,1)} %copy-done.8) | copy-start | bytes 3145732
  207.3 1.5 copy-start.3
  209.0 22.9 %copy-start.10 = (bf16[1280,2048]{0,1:T(8,128)(2,1)}, bf16[1280,2048]{0,1:T(8,128)(2,1)S(1)}, u32[]{:S(2)}) copy-start(bf16[1280,2048]{0,1:T(8,128)(2,1)S(1)} %constant_dynamic-update-slice_fusion.5) | copy-start | bytes 15728644
  209.0 21.8 %copy-start.7 = (bf16[256,2048]{1,0:T(8,128)(2,1)S(1)}, bf16[256,2048]{1,0:T(8,128)(2,1)}, u32[]{:S(2)}) copy-start(bf16[256,2048]{1,0:T(8,128)(2,1)} %copy-done.6) | copy-start | bytes 3145732
  230.7 3.4 %copy-start.1 = (bf16[256,2048]{1,0:T(8,128)(2,1)S(1)}, bf16[256,2048]{1,0:T(8,128)(2,1)}, u32[]{:S(2)}) copy-start(bf16[256,2048]{1,0:T(8,128)(2,1)} %param.11) | copy-start | bytes 3145732
  235.2 8.0 %copy-start.5 = (bf16[256,2048]{0,1:T(8,128)(2,1)S(1)}, bf16[256,2048]{0,1:T(8,128)(2,1)}, u32[]{:S(2)}) copy-start(bf16[256,2048]{0,1:T(8,128)(2,1)} %copy.26) | copy-start | bytes 3145732
  277.2 1.8 copy-start.11
  277.2 1.8 copy-start.12
Sparse Core Ops, SparseCore 0:
  15.0 63.6 all-gather.2
where the time goes:
time: 291 us; the launch traced here: 289 us
  waiting for transfers between devices  182 us (63%)
  matrix products  42.9 us (15%)
  local copies, waits for them, and re-layouts  28 us (10%)
  between operations  13.7 us (5%)
  other arithmetic  11.9 us (4%)
  starting transfers between devices  10.4 us (4%)
    ppermute x8, waiting for transfers between devices, passed_along(): lax.ppermute(value, axis, [(source, source + steps) for source in range(l...  182 us
    dot_general x4, matrix products, attend(): jnp.einsum('gts,sge->tge', weights, value_group, preferred_element_type=j...  19.2 us
    unnamed x36, local copies, waits for them, and re-layouts  16.1 us
    sub x4, matrix products, attend(): expos = jnp.exp(scores - peak)  13.1 us
    ppermute x8, starting transfers between devices, passed_along(): lax.ppermute(value, axis, [(source, source + steps) for source in range(l...  10.4 us
    concatenate x2, local copies, waits for them, and re-layouts, shards(): window_values = jnp.concatenate([member[1] for member in ordered], axis=0)  9.01 us
    select_n x4, other arithmetic, lap(): return jnp.where(reached, new, before)  6.47 us
  transfers between devices with their start and end apart: 9, of which 8 were waited for; matrix products, arithmetic and copies ran while one was open for 9% of the time, Pallas kernels for 0%

commit v1 on v0

--- a/solution.py
+++ b/solution.py
@@ -1,12 +1,16 @@
+import functools
 import math
 
 import jax
 import jax.numpy as jnp
 from jax import lax
+from jax.experimental import pallas as pl
+from jax.experimental.pallas import tpu as pltpu
 from jax.sharding import PartitionSpec as P
 
 HEAD = 128
 WINDOW = 1024
+EPS = 1e-05
 
 
 def passed_along(value, axis, steps):
@@ -84,7 +88,7 @@
         attend, (split_groups(queries), split_groups(window_keys), split_groups(window_values))
     )
     attended = jnp.moveaxis(attended, 0, 1).reshape(tok_rows, head_count, HEAD)
-    windowed = attended * lax.rsqrt(jnp.mean(attended * attended, axis=-1, keepdims=True) + 1e-05)
+    windowed = attended * lax.rsqrt(jnp.mean(attended * attended, axis=-1, keepdims=True) + EPS)
     windowed = windowed * window_gain.reshape(head_count, HEAD)
     phi_query = feature_map(queries).reshape(tok_rows, head_count, HEAD)
     phi_key = feature_map(key_vectors).reshape(tok_rows, head_count, HEAD)
@@ -104,14 +108,311 @@
         "hts,shf->thf", affinity, value_heads, preferred_element_type=jnp.float32
     )
     linear = from_state + local_part
-    normed = linear * lax.rsqrt(jnp.mean(linear * linear, axis=-1, keepdims=True) + 1e-05)
+    normed = linear * lax.rsqrt(jnp.mean(linear * linear, axis=-1, keepdims=True) + EPS)
     normed = normed * norm_gain.reshape(head_count, HEAD)
     return (windowed + normed).reshape(tok_rows, model_width).astype(jnp.bfloat16)
 
 
+QA, QB, KK, VV, OA, OB, ST, SN = range(8)
+EXP_SCALE = math.log2(math.e) / math.sqrt(HEAD)
+LOW = -1e30
+
+
+def nt(a, b):
+    return lax.dot_general(a, b, (((1,), (1,)), ((), ())), preferred_element_type=jnp.float32)
+
+
+def tn(a, b):
+    return lax.dot_general(a, b, (((0,), (0,)), ((), ())), preferred_element_type=jnp.float32)
+
+
+def tt(a, b):
+    return lax.dot_general(a, b, (((0,), (1,)), ((), ())), preferred_element_type=jnp.float32)
+
+
+def hub_kernel(
+    n,
+    q_ref, k_ref, v_ref, gn_ref, gw_ref, out_ref,
+    qa, qb, kr, vr, oa_s, ob_s, st_s, sn_s, oa_r, ob_r, st_r, sn_r,
+    send, recv,
+):
+    tok, width = q_ref.shape
+    heads = width // HEAD
+    me = lax.axis_index("ctx")
+    left, right = me - 1, me + 1
+    first, hub, last = 0, 1, n - 1
+
+    def cols(h):
+        return pl.ds(pl.multiple_of(h * HEAD, HEAD), HEAD)
+
+    def move(stream, src, dst, h, target):
+        return pltpu.make_async_remote_copy(
+            src_ref=src,
+            dst_ref=dst,
+            send_sem=send.at[stream, h],
+            recv_sem=recv.at[stream, h],
+            device_id={"ctx": target},
+            device_id_type=pl.DeviceIdType.MESH,
+        )
+
+    def q_left(h):
+        return move(QA, q_ref.at[:, cols(h)], qa.at[:, cols(h)], h, left)
+
+    def q_relay(h):
+        return move(QB, qa.at[:, cols(h)], qb.at[:, cols(h)], h, left)
+
+    def k_right(h):
+        return move(KK, k_ref.at[:, cols(h)], kr.at[:, cols(h)], h, right)
+
+    def v_right(h):
+        return move(VV, v_ref.at[:, cols(h)], vr.at[:, cols(h)], h, right)
+
+    def oa_right(h):
+        return move(OA, oa_s.at[h], oa_r.at[h], h, right)
+
+    def ob_right(h):
+        return move(OB, ob_s.at[h], ob_r.at[h], h, right)
+
+    def st_right(h):
+        return move(ST, st_s.at[h], st_r.at[h], h, right)
+
+    def sn_right(h):
+        return move(SN, sn_s.at[h], sn_r.at[h], h, right)
+
+    def each_head(body):
+        def step(h, carry):
+            body(h)
+            return carry
+
+        lax.fori_loop(0, heads, step, 0)
+
+    barrier = pltpu.get_barrier_semaphore()
+
+    @pl.when(me > first)
+    def _():
+        pl.semaphore_signal(
+            barrier, inc=1, device_id={"ctx": left}, device_id_type=pl.DeviceIdType.MESH
+        )
+
+    @pl.when(me < last)
+    def _():
+        pl.semaphore_signal(
+            barrier, inc=1, device_id={"ctx": right}, device_id_type=pl.DeviceIdType.MESH
+        )
+
+    peers = (me > first).astype(jnp.int32) + (me < last).astype(jnp.int32)
+    pl.semaphore_wait(barrier, peers)
+
+    key_at = lax.broadcasted_iota(jnp.int32, (tok, tok), 0)
+    query_at = lax.broadcasted_iota(jnp.int32, (tok, tok), 1)
+    causal = key_at <= query_at
+
+    def soft(scores, values):
+        peak = functools.reduce(
+            jnp.maximum, [jnp.max(s, axis=0, keepdims=True) for s in scores]
+        )
+        total, out = 0.0, 0.0
+        for s, v in zip(scores, values):
+            e = jnp.exp2((s - peak) * EXP_SCALE)
+            total = total + jnp.sum(e, axis=0, keepdims=True)
+            out = out + tn(v, e.astype(jnp.bfloat16))
+        return peak, total, out
+
+    def merge(one, peak, total, out):
+        top = jnp.maximum(one[0], peak)
+        f1 = jnp.exp2((one[0] - top) * EXP_SCALE)
+        f2 = jnp.exp2((peak - top) * EXP_SCALE)
+        return top, one[1] * f1 + total * f2, one[2] * f1 + out.astype(jnp.float32) * f2
+
+    def local_linear(q, phi_k, v):
+        phi_q = feature_map(q)
+        affinity = jnp.where(causal, nt(phi_k, phi_q), 0.0).astype(jnp.bfloat16)
+        return phi_q, tn(v, affinity)
+
+    def finish(h, soft_sum, linear):
+        _, total, out = soft_sum
+        att = out * (1.0 / total)
+        att = att * lax.rsqrt(jnp.mean(att * att, axis=0, keepdims=True) + EPS)
+        lin = linear * lax.rsqrt(jnp.mean(linear * linear, axis=0, keepdims=True) + EPS)
+        row = att.T * gw_ref[pl.ds(h, 1), :] + lin.T * gn_ref[pl.ds(h, 1), :]
+        out_ref[:, cols(h)] = row.astype(jnp.bfloat16)
+
+    def diagonal(q, k):
+        return jnp.where(causal, nt(k, q), LOW)
+
+    @pl.when(me == first)
+    def _():
+        def start(h):
+            k_right(h).start()
+            v_right(h).start()
+
+        each_head(start)
+
+        def compute(h):
+            q, k, v = q_ref[:, cols(h)], k_ref[:, cols(h)], v_ref[:, cols(h)]
+            _, linear = local_linear(q, feature_map(k), v)
+            finish(h, soft([diagonal(q, k)], [v]), linear)
+
+        each_head(compute)
+
+        def drain(h):
+            k_right(h).wait_send()
+            v_right(h).wait_send()
+
+        each_head(drain)
+
+    @pl.when(me == hub)
+    def _():
+        def compute(h):
+            k_right(h).wait_recv()
+            v_right(h).wait_recv()
+            q_left(h).wait_recv()
+            q_relay(h).wait_recv()
+            q, k, v = q_ref[:, cols(h)], k_ref[:, cols(h)], v_ref[:, cols(h)]
+            k0, v0 = kr[:, cols(h)], vr[:, cols(h)]
+            q2, q3 = qa[:, cols(h)], qb[:, cols(h)]
+            peak, total, out = soft([nt(k0, q3), nt(k, q3)], [v0, v])
+            ob_s[h] = out.astype(jnp.bfloat16)
+            st_s[h, 2:3] = peak
+            st_s[h, 3:4] = total
+            peak, total, out = soft([nt(k0, q2), nt(k, q2)], [v0, v])
+            oa_s[h] = out.astype(jnp.bfloat16)
+            st_s[h, 0:1] = peak
+            st_s[h, 1:2] = total
+            phi_k = feature_map(k)
+            before = tn(feature_map(k0), v0)
+            sn_s[h] = (before + tn(phi_k, v)).astype(jnp.bfloat16)
+            st_right(h).start()
+            ob_right(h).start()
+            sn_right(h).start()
+            oa_right(h).start()
+            phi_q, linear = local_linear(q, phi_k, v)
+            linear = linear + tt(before.astype(jnp.bfloat16), phi_q)
+            finish(h, soft([nt(k0, q), diagonal(q, k)], [v0, v]), linear)
+
+        each_head(compute)
+
+        def drain(h):
+            st_right(h).wait_send()
+            ob_right(h).wait_send()
+            sn_right(h).wait_send()
+            oa_right(h).wait_send()
+
+        each_head(drain)
+
+    @pl.when((me > hub) & (me < last))
+    def _():
+        def relay(h):
+            q_left(h).start()
+            q_left(h).wait_recv()
+            q_relay(h).start()
+
+        each_head(relay)
+
+        def compute(h):
+            q, k, v = q_ref[:, cols(h)], k_ref[:, cols(h)], v_ref[:, cols(h)]
+            phi_k = feature_map(k)
+            phi_q, linear = local_linear(q, phi_k, v)
+            state = tn(phi_k, v)
+            other = soft([nt(k, qa[:, cols(h)])], [v])
+            own = soft([diagonal(q, k)], [v])
+            st_right(h).wait_recv()
+            ob_right(h).wait_recv()
+            stats = st_r[h]
+            peak, total, out = merge(other, stats[2:3], stats[3:4], ob_r[h])
+            oa_s[h] = out.astype(jnp.bfloat16)
+            st_s[h, 0:1] = peak
+            st_s[h, 1:2] = total
+            st_s[h, 2:3] = peak
+            st_s[h, 3:4] = total
+            st_right(h).start()
+            oa_right(h).start()
+            sn_right(h).wait_recv()
+            carried = sn_r[h]
+            sn_s[h] = (carried.astype(jnp.float32) + state).astype(jnp.bfloat16)
+            sn_right(h).start()
+            linear = linear + tt(carried, phi_q)
+            oa_right(h).wait_recv()
+            finish(h, merge(own, stats[0:1], stats[1:2], oa_r[h]), linear)
+
+        each_head(compute)
+
+        def drain(h):
+            q_left(h).wait_send()
+            q_relay(h).wait_send()
+            st_right(h).wait_send()
+            oa_right(h).wait_send()
+            sn_right(h).wait_send()
+
+        each_head(drain)
+
+    @pl.when(me == last)
+    def _():
+        def start(h):
+            q_left(h).start()
+
+        each_head(start)
+
+        def compute(h):
+            q, k, v = q_ref[:, cols(h)], k_ref[:, cols(h)], v_ref[:, cols(h)]
+            phi_q, linear = local_linear(q, feature_map(k), v)
+            own = soft([diagonal(q, k)], [v])
+            st_right(h).wait_recv()
+            sn_right(h).wait_recv()
+            linear = linear + tt(sn_r[h], phi_q)
+            stats = st_r[h]
+            oa_right(h).wait_recv()
+            finish(h, merge(own, stats[0:1], stats[1:2], oa_r[h]), linear)
+
+        each_head(compute)
+
+        def drain(h):
+            q_left(h).wait_send()
+
+        each_head(drain)
+
+
+def hub_shards(n, queries, key_vectors, value_vectors, norm_gain, window_gain):
+    tok, width = queries.shape
+    heads = width // HEAD
+    vmem = pl.BlockSpec(memory_space=pltpu.VMEM)
+    block = pltpu.VMEM((tok, width), jnp.bfloat16)
+    partial = pltpu.VMEM((heads, HEAD, tok), jnp.bfloat16)
+    stats = pltpu.VMEM((heads, 4, tok), jnp.float32)
+    state = pltpu.VMEM((heads, HEAD, HEAD), jnp.bfloat16)
+    return pl.pallas_call(
+        functools.partial(hub_kernel, n),
+        out_shape=jax.ShapeDtypeStruct((tok, width), jnp.bfloat16),
+        in_specs=[vmem] * 5,
+        out_specs=vmem,
+        scratch_shapes=[block] * 4
+        + [partial, partial, stats, state] * 2
+        + [pltpu.SemaphoreType.DMA((8, heads)), pltpu.SemaphoreType.DMA((8, heads))],
+        compiler_params=pltpu.CompilerParams(
+            collective_id=0, has_side_effects=True, vmem_limit_bytes=56 * 2**20
+        ),
+        name="hub_attention",
+    )(
+        queries,
+        key_vectors,
+        value_vectors,
+        norm_gain.reshape(heads, HEAD),
+        window_gain.reshape(heads, HEAD),
+    )
+
+
 def solution(mesh):
+    count = mesh.shape["ctx"]
+
+    def run(queries, key_vectors, value_vectors, norm_gain, window_gain):
+        args = (queries, key_vectors, value_vectors, norm_gain, window_gain)
+        fits = count * queries.shape[0] <= WINDOW
+        if fits and count - 2 == 2:
+            return hub_shards(count, *args)
+        return shards(*args)
+
     return jax.shard_map(
-        shards,
+        run,
         mesh=mesh,
         in_specs=(P(("dp", "ctx"), None), P(("dp", "ctx"), None), P(("dp", "ctx"), None), P(), P()),
         out_specs=P(("dp", "ctx"), None),

time: 291 us -> 76.6 us (0.26)
  waiting for transfers between devices: 182 us -> 0 us
  Pallas kernels: 0 us -> 74.1 us
  matrix products: 42.9 us -> 0 us
  local copies, waits for them, and re-layouts: 28 us -> 2.3 us
  between operations: 13.7 us -> 0.01 us
  other arithmetic: 11.9 us -> 0 us
  starting transfers between devices: 10.4 us -> 0 us
    ppermute x8 -> x0, waiting for transfers between devices: 182 us -> none  [passed_along(): lax.ppermute(value, axis, [(source, source + steps) for source in range(l...]
    pallas_call x0 -> x1, Pallas kernels: none -> 74.1 us  [hub_shards(): pl.pallas_call(functools.partial(hub_kernel, n), out_shape=jax.ShapeDtype...]
    dot_general x7 -> x0, matrix products: 29.7 us -> none  [the longest x4 19.2 us: attend(): jnp.einsum('gts,sge->tge', weights, value_group, preferred_element_type=j...]
    unnamed x36 -> x1, local copies, waits for them, and re-layouts: 16.1 us -> 2.3 us
    sub x4 -> x0, matrix products: 13.1 us -> none  [attend(): expos = jnp.exp(scores - peak)]
    ppermute x8 -> x0, starting transfers between devices: 10.4 us -> none  [passed_along(): lax.ppermute(value, axis, [(source, source + steps) for source in range(l...]
    concatenate x3 -> x0, local copies, waits for them, and re-layouts: 9.08 us -> none  [the longest x2 9.01 us: shards(): window_values = jnp.concatenate([member[1] for member in ordered], axis=0)]
    select_n x4 -> x0, other arithmetic: 6.47 us -> none  [lap(): return jnp.where(reached, new, before)]
  transfers between devices with their start and end apart: 9 -> 0, of which waited for: 8 -> 0; matrix products, arithmetic and copies ran while one was open for 9% -> 0% of each run, Pallas kernels for 0% -> 0%
where the time goes in v1:
time: 76.6 us; the launch traced here: 76.4 us
  Pallas kernels  74.1 us (97%)
  local copies, waits for them, and re-layouts  2.3 us (3%)
    pallas_call x1, Pallas kernels, hub_shards(): pl.pallas_call(functools.partial(hub_kernel, n), out_shape=jax.ShapeDtype...  74.1 us
    unnamed x1, local copies, waits for them, and re-layouts  2.3 us

profile of v1, /device:TPU:30, one launch (start us, length us, event | category | flops | bytes accessed | tf_op | source)
XLA Modules:
  0.0 76.4 jit_solution(17269932937820096960)
XLA Ops:
  0.0 74.1 %hub_attention.1 = bf16[256,2048]{1,0:T(8,128)(2,1)} custom-call(bf16[256,2048]{1,0:T(8,128)(2,1)} %q_ref.1, bf16[256,2048]{1,0:T(8,128)(2,1)} %k_ref.1, bf16[256,2048]{1,0:T(8,128)(2,1)} %v_ref.1, f32[16,128]{1,0:T(8,128)} %bitcast.2, f32[16,128]{1,0:T(8,128)} %bitcast.3), custom_call_target="tpu_custom_call" | custom-call | tf_op jit(solution)/shard_map/hub_attention/pallas_call | solution.py:383
  74.1 2.3 %copy.7 = bf16[256,2048]{1,0:T(8,128)(2,1)} copy(bf16[256,2048]{1,0:T(8,128)(2,1)} %hub_attention.1) | data formatting | bytes 2097152

commit v2 on v1

--- a/solution.py
+++ b/solution.py
@@ -134,7 +134,7 @@
     n,
     q_ref, k_ref, v_ref, gn_ref, gw_ref, out_ref,
     qa, qb, kr, vr, oa_s, ob_s, st_s, sn_s, oa_r, ob_r, st_r, sn_r,
-    send, recv,
+    q_own, k_own, v_own, mixed, send, recv, loaded, stored,
 ):
     tok, width = q_ref.shape
     heads = width // HEAD
@@ -186,6 +186,16 @@
 
         lax.fori_loop(0, heads, step, 0)
 
+    loads = [
+        pltpu.make_async_copy(src, dst, loaded.at[i])
+        for i, (src, dst) in enumerate([(k_ref, k_own), (v_ref, v_own), (q_ref, q_own)])
+    ]
+    for load in loads:
+        load.start()
+
+    def store(h):
+        return pltpu.make_async_copy(mixed.at[:, cols(h)], out_ref.at[:, cols(h)], stored.at[h])
+
     barrier = pltpu.get_barrier_semaphore()
 
     @pl.when(me > first)
@@ -218,11 +228,15 @@
             out = out + tn(v, e.astype(jnp.bfloat16))
         return peak, total, out
 
-    def merge(one, peak, total, out):
-        top = jnp.maximum(one[0], peak)
+    def normalised(soft_sum):
+        peak, total, out = soft_sum
+        return peak + jnp.log2(total) * (1.0 / EXP_SCALE), out * (1.0 / total)
+
+    def merge(one, level, out):
+        top = jnp.maximum(one[0], level)
         f1 = jnp.exp2((one[0] - top) * EXP_SCALE)
-        f2 = jnp.exp2((peak - top) * EXP_SCALE)
-        return top, one[1] * f1 + total * f2, one[2] * f1 + out.astype(jnp.float32) * f2
+        f2 = jnp.exp2((level - top) * EXP_SCALE)
+        return top, one[1] * f1 + f2, one[2] * f1 + out.astype(jnp.float32) * f2
 
     def local_linear(q, phi_k, v):
         phi_q = feature_map(q)
@@ -235,7 +249,8 @@
         att = att * lax.rsqrt(jnp.mean(att * att, axis=0, keepdims=True) + EPS)
         lin = linear * lax.rsqrt(jnp.mean(linear * linear, axis=0, keepdims=True) + EPS)
         row = att.T * gw_ref[pl.ds(h, 1), :] + lin.T * gn_ref[pl.ds(h, 1), :]
-        out_ref[:, cols(h)] = row.astype(jnp.bfloat16)
+        mixed[:, cols(h)] = row.astype(jnp.bfloat16)
+        store(h).start()
 
     def diagonal(q, k):
         return jnp.where(causal, nt(k, q), LOW)
@@ -248,8 +263,11 @@
 
         each_head(start)
 
+        for load in loads:
+            load.wait()
+
         def compute(h):
-            q, k, v = q_ref[:, cols(h)], k_ref[:, cols(h)], v_ref[:, cols(h)]
+            q, k, v = q_own[:, cols(h)], k_own[:, cols(h)], v_own[:, cols(h)]
             _, linear = local_linear(q, feature_map(k), v)
             finish(h, soft([diagonal(q, k)], [v]), linear)
 
@@ -263,34 +281,46 @@
 
     @pl.when(me == hub)
     def _():
-        def compute(h):
+        for load in loads:
+            load.wait()
+
+        def compute(h, later_first):
+            q, k, v = q_own[:, cols(h)], k_own[:, cols(h)], v_own[:, cols(h)]
+            phi_k = feature_map(k)
+            state = tn(phi_k, v)
             k_right(h).wait_recv()
             v_right(h).wait_recv()
-            q_left(h).wait_recv()
-            q_relay(h).wait_recv()
-            q, k, v = q_ref[:, cols(h)], k_ref[:, cols(h)], v_ref[:, cols(h)]
             k0, v0 = kr[:, cols(h)], vr[:, cols(h)]
-            q2, q3 = qa[:, cols(h)], qb[:, cols(h)]
-            peak, total, out = soft([nt(k0, q3), nt(k, q3)], [v0, v])
-            ob_s[h] = out.astype(jnp.bfloat16)
-            st_s[h, 2:3] = peak
-            st_s[h, 3:4] = total
-            peak, total, out = soft([nt(k0, q2), nt(k, q2)], [v0, v])
-            oa_s[h] = out.astype(jnp.bfloat16)
-            st_s[h, 0:1] = peak
-            st_s[h, 1:2] = total
-            phi_k = feature_map(k)
             before = tn(feature_map(k0), v0)
-            sn_s[h] = (before + tn(phi_k, v)).astype(jnp.bfloat16)
+            sn_s[h] = (before + state).astype(jnp.bfloat16)
+            sn_right(h).start()
+
+            def part(arrival, queries, row, target, sending):
+                arrival(h).wait_recv()
+                other = queries[:, cols(h)]
+                level, out = normalised(soft([nt(k0, other), nt(k, other)], [v0, v]))
+                target[h] = out.astype(jnp.bfloat16)
+                st_s[h, row : row + 1] = level
+                return sending(h)
+
+            part_a = (q_left, qa, 0, oa_s, oa_right)
+            part_b = (q_relay, qb, 1, ob_s, ob_right)
+            order = (part_b, part_a) if later_first else (part_a, part_b)
+            part(*order[0]).start()
+            second = part(*order[1])
             st_right(h).start()
-            ob_right(h).start()
-            sn_right(h).start()
-            oa_right(h).start()
+            second.start()
             phi_q, linear = local_linear(q, phi_k, v)
             linear = linear + tt(before.astype(jnp.bfloat16), phi_q)
             finish(h, soft([nt(k0, q), diagonal(q, k)], [v0, v]), linear)
 
-        each_head(compute)
+        compute(0, False)
+
+        def step(h, carry):
+            compute(h, True)
+            return carry
+
+        lax.fori_loop(1, heads, step, 0)
 
         def drain(h):
             st_right(h).wait_send()
@@ -309,31 +339,31 @@
 
         each_head(relay)
 
+        for load in loads:
+            load.wait()
+
         def compute(h):
-            q, k, v = q_ref[:, cols(h)], k_ref[:, cols(h)], v_ref[:, cols(h)]
+            q, k, v = q_own[:, cols(h)], k_own[:, cols(h)], v_own[:, cols(h)]
             phi_k = feature_map(k)
             phi_q, linear = local_linear(q, phi_k, v)
             state = tn(phi_k, v)
             other = soft([nt(k, qa[:, cols(h)])], [v])
             own = soft([diagonal(q, k)], [v])
-            st_right(h).wait_recv()
-            ob_right(h).wait_recv()
-            stats = st_r[h]
-            peak, total, out = merge(other, stats[2:3], stats[3:4], ob_r[h])
-            oa_s[h] = out.astype(jnp.bfloat16)
-            st_s[h, 0:1] = peak
-            st_s[h, 1:2] = total
-            st_s[h, 2:3] = peak
-            st_s[h, 3:4] = total
-            st_right(h).start()
-            oa_right(h).start()
             sn_right(h).wait_recv()
             carried = sn_r[h]
             sn_s[h] = (carried.astype(jnp.float32) + state).astype(jnp.bfloat16)
             sn_right(h).start()
             linear = linear + tt(carried, phi_q)
+            st_right(h).wait_recv()
+            ob_right(h).wait_recv()
+            level, out = normalised(merge(other, st_r[h, 1:2], ob_r[h]))
+            oa_s[h] = out.astype(jnp.bfloat16)
+            st_s[h, 0:1] = level
+            st_s[h, 1:2] = level
+            st_right(h).start()
+            oa_right(h).start()
             oa_right(h).wait_recv()
-            finish(h, merge(own, stats[0:1], stats[1:2], oa_r[h]), linear)
+            finish(h, merge(own, st_r[h, 0:1], oa_r[h]), linear)
 
         each_head(compute)
 
@@ -353,16 +383,18 @@
 
         each_head(start)
 
+        for load in loads:
+            load.wait()
+
         def compute(h):
-            q, k, v = q_ref[:, cols(h)], k_ref[:, cols(h)], v_ref[:, cols(h)]
+            q, k, v = q_own[:, cols(h)], k_own[:, cols(h)], v_own[:, cols(h)]
             phi_q, linear = local_linear(q, feature_map(k), v)
             own = soft([diagonal(q, k)], [v])
-            st_right(h).wait_recv()
             sn_right(h).wait_recv()
             linear = linear + tt(sn_r[h], phi_q)
-            stats = st_r[h]
+            st_right(h).wait_recv()
             oa_right(h).wait_recv()
-            finish(h, merge(own, stats[0:1], stats[1:2], oa_r[h]), linear)
+            finish(h, merge(own, st_r[h, 0:1], oa_r[h]), linear)
 
         each_head(compute)
 
@@ -370,24 +402,71 @@
             q_left(h).wait_send()
 
         each_head(drain)
+
+    def settle(h):
+        store(h).wait()
+
+    each_head(settle)
+
+
+def copy_kernel(chunks, src_ref, dst_ref, held, arrived, left):
+    rows = held.shape[0] // chunks
+    into = [
+        pltpu.make_async_copy(
+            src_ref.at[pl.ds(i * rows, rows)], held.at[pl.ds(i * rows, rows)], arrived.at[i]
+        )
+        for i in range(chunks)
+    ]
+    out = [
+        pltpu.make_async_copy(
+            held.at[pl.ds(i * rows, rows)], dst_ref.at[pl.ds(i * rows, rows)], left.at[i]
+        )
+        for i in range(chunks)
+    ]
+    for one in into:
+        one.start()
+    for one, other in zip(into, out):
+        one.wait()
+        other.start()
+    for other in out:
+        other.wait()
+
+
+def copied(array, chunks=4):
+    hbm = pl.BlockSpec(memory_space=pl.ANY)
+    return pl.pallas_call(
+        functools.partial(copy_kernel, chunks),
+        out_shape=jax.ShapeDtypeStruct(array.shape, array.dtype),
+        in_specs=[hbm],
+        out_specs=hbm,
+        scratch_shapes=[
+            pltpu.VMEM(array.shape, array.dtype),
+            pltpu.SemaphoreType.DMA((chunks,)),
+            pltpu.SemaphoreType.DMA((chunks,)),
+        ],
+        name="result_copy",
+    )(array)
 
 
 def hub_shards(n, queries, key_vectors, value_vectors, norm_gain, window_gain):
     tok, width = queries.shape
     heads = width // HEAD
     vmem = pl.BlockSpec(memory_space=pltpu.VMEM)
+    hbm = pl.BlockSpec(memory_space=pl.ANY)
     block = pltpu.VMEM((tok, width), jnp.bfloat16)
     partial = pltpu.VMEM((heads, HEAD, tok), jnp.bfloat16)
-    stats = pltpu.VMEM((heads, 4, tok), jnp.float32)
+    stats = pltpu.VMEM((heads, 2, tok), jnp.float32)
     state = pltpu.VMEM((heads, HEAD, HEAD), jnp.bfloat16)
     return pl.pallas_call(
         functools.partial(hub_kernel, n),
         out_shape=jax.ShapeDtypeStruct((tok, width), jnp.bfloat16),
-        in_specs=[vmem] * 5,
-        out_specs=vmem,
+        in_specs=[hbm] * 3 + [vmem] * 2,
+        out_specs=hbm,
         scratch_shapes=[block] * 4
         + [partial, partial, stats, state] * 2
-        + [pltpu.SemaphoreType.DMA((8, heads)), pltpu.SemaphoreType.DMA((8, heads))],
+        + [block] * 4
+        + [pltpu.SemaphoreType.DMA((8, heads)), pltpu.SemaphoreType.DMA((8, heads))]
+        + [pltpu.SemaphoreType.DMA((3,)), pltpu.SemaphoreType.DMA((heads,))],
         compiler_params=pltpu.CompilerParams(
             collective_id=0, has_side_effects=True, vmem_limit_bytes=56 * 2**20
         ),
@@ -408,7 +487,7 @@
         args = (queries, key_vectors, value_vectors, norm_gain, window_gain)
         fits = count * queries.shape[0] <= WINDOW
         if fits and count - 2 == 2:
-            return hub_shards(count, *args)
+            return copied(hub_shards(count, *args))
         return shards(*args)
 
     return jax.shard_map(

time: 76.6 us -> 72.7 us (0.949)
  local copies, waits for them, and re-layouts: 2.3 us -> 0 us
  Pallas kernels: 74.1 us -> 72.5 us
    pallas_call x1, Pallas kernels: 74.1 us -> 70.5 us  [hub_shards(): pl.pallas_call(functools.partial(hub_kernel, n), out_shape=jax.ShapeDtype...]
    unnamed x1 -> x0, local copies, waits for them, and re-layouts: 2.3 us -> none
    pallas_call x0 -> x1, Pallas kernels: none -> 1.98 us  [copied(): pl.pallas_call(functools.partial(copy_kernel, chunks), out_shape=jax.Shap...]
where the time goes in v2:
time: 72.7 us; the launch traced here: 72.5 us
  Pallas kernels  72.5 us (100%)
    pallas_call x1, Pallas kernels, hub_shards(): pl.pallas_call(functools.partial(hub_kernel, n), out_shape=jax.ShapeDtype...  70.5 us
    pallas_call x1, Pallas kernels, copied(): pl.pallas_call(functools.partial(copy_kernel, chunks), out_shape=jax.Shap...  1.98 us

profile of v2, /device:TPU:30, one launch (start us, length us, event | category | flops | bytes accessed | tf_op | source)
XLA Modules:
  0.0 72.5 jit_solution(7578132793663730303)
XLA Ops:
  0.0 70.5 %hub_attention.1.src_ref = bf16[256,2048]{1,0:T(8,128)(2,1)} custom-call(bf16[256,2048]{1,0:T(8,128)(2,1)} %q_ref.1, bf16[256,2048]{1,0:T(8,128)(2,1)} %k_ref.1, bf16[256,2048]{1,0:T(8,128)(2,1)} %v_ref.1, f32[16,128]{1,0:T(8,128)} %bitcast.2, f32[16,128]{1,0:T(8,128)} %bitcast.3), custom_call_target="tpu_custom_call" | custom-call | tf_op jit(solution)/shard_map/hub_attention/pallas_call | solution.py:460
  70.5 2.0 %result_copy.1 = bf16[256,2048]{1,0:T(8,128)(2,1)} custom-call(bf16[256,2048]{1,0:T(8,128)(2,1)} %hub_attention.1.src_ref), custom_call_target="tpu_custom_call" | custom-call | tf_op jit(solution)/shard_map/result_copy/pallas_call | solution.py:437

commit v3 on v2

--- a/solution.py
+++ b/solution.py
@@ -305,11 +305,19 @@
 
             part_a = (q_left, qa, 0, oa_s, oa_right)
             part_b = (q_relay, qb, 1, ob_s, ob_right)
-            order = (part_b, part_a) if later_first else (part_a, part_b)
-            part(*order[0]).start()
-            second = part(*order[1])
-            st_right(h).start()
-            second.start()
+            if later_first:
+                part(*part_b).start()
+
+                @pl.when(h > 1)
+                def _():
+                    oa_right(h - 1).start()
+
+                part(*part_a)
+                st_right(h).start()
+            else:
+                part(*part_a).start()
+                part(*part_b).start()
+                st_right(h).start()
             phi_q, linear = local_linear(q, phi_k, v)
             linear = linear + tt(before.astype(jnp.bfloat16), phi_q)
             finish(h, soft([nt(k0, q), diagonal(q, k)], [v0, v]), linear)
@@ -321,6 +329,7 @@
             return carry
 
         lax.fori_loop(1, heads, step, 0)
+        oa_right(heads - 1).start()
 
         def drain(h):
             st_right(h).wait_send()
@@ -342,7 +351,7 @@
         for load in loads:
             load.wait()
 
-        def compute(h):
+        def front(h):
             q, k, v = q_own[:, cols(h)], k_own[:, cols(h)], v_own[:, cols(h)]
             phi_k = feature_map(k)
             phi_q, linear = local_linear(q, phi_k, v)
@@ -362,10 +371,19 @@
             st_s[h, 1:2] = level
             st_right(h).start()
             oa_right(h).start()
+            return own, linear
+
+        def back(h, held):
+            own, linear = held
             oa_right(h).wait_recv()
             finish(h, merge(own, st_r[h, 0:1], oa_r[h]), linear)
 
-        each_head(compute)
+        def step(h, held):
+            ahead = front(h)
+            back(h - 1, held)
+            return ahead
+
+        back(heads - 1, lax.fori_loop(1, heads, step, front(0)))
 
         def drain(h):
             q_left(h).wait_send()

time: 72.7 us -> 73.1 us (level)
  no operation moved by 1% of the time
where the time goes in v3:
time: 73.1 us; the launch traced here: 72.8 us
  Pallas kernels  72.8 us (100%)
    pallas_call x1, Pallas kernels, hub_shards(): pl.pallas_call(functools.partial(hub_kernel, n), out_shape=jax.ShapeDtype...  70.8 us
    pallas_call x1, Pallas kernels, copied(): pl.pallas_call(functools.partial(copy_kernel, chunks), out_shape=jax.Shap...  1.98 us

profile of v3, /device:TPU:30, one launch (start us, length us, event | category | flops | bytes accessed | tf_op | source)
XLA Modules:
  0.0 72.8 jit_solution(15147961238577080956)
XLA Ops:
  0.0 70.8 %hub_attention.1.src_ref = bf16[256,2048]{1,0:T(8,128)(2,1)} custom-call(bf16[256,2048]{1,0:T(8,128)(2,1)} %q_ref.1, bf16[256,2048]{1,0:T(8,128)(2,1)} %k_ref.1, bf16[256,2048]{1,0:T(8,128)(2,1)} %v_ref.1, f32[16,128]{1,0:T(8,128)} %bitcast.2, f32[16,128]{1,0:T(8,128)} %bitcast.3), custom_call_target="tpu_custom_call" | custom-call | tf_op jit(solution)/shard_map/hub_attention/pallas_call | solution.py:478
  70.8 2.0 %result_copy.1 = bf16[256,2048]{1,0:T(8,128)(2,1)} custom-call(bf16[256,2048]{1,0:T(8,128)(2,1)} %hub_attention.1.src_ref), custom_call_target="tpu_custom_call" | custom-call | tf_op jit(solution)/shard_map/result_copy/pallas_call | solution.py:455

commit v4 on v2

--- a/solution.py
+++ b/solution.py
@@ -134,7 +134,7 @@
     n,
     q_ref, k_ref, v_ref, gn_ref, gw_ref, out_ref,
     qa, qb, kr, vr, oa_s, ob_s, st_s, sn_s, oa_r, ob_r, st_r, sn_r,
-    q_own, k_own, v_own, mixed, send, recv, loaded, stored,
+    q_own, k_own, v_own, send, recv, loaded,
 ):
     tok, width = q_ref.shape
     heads = width // HEAD
@@ -192,9 +192,6 @@
     ]
     for load in loads:
         load.start()
-
-    def store(h):
-        return pltpu.make_async_copy(mixed.at[:, cols(h)], out_ref.at[:, cols(h)], stored.at[h])
 
     barrier = pltpu.get_barrier_semaphore()
 
@@ -249,8 +246,7 @@
         att = att * lax.rsqrt(jnp.mean(att * att, axis=0, keepdims=True) + EPS)
         lin = linear * lax.rsqrt(jnp.mean(linear * linear, axis=0, keepdims=True) + EPS)
         row = att.T * gw_ref[pl.ds(h, 1), :] + lin.T * gn_ref[pl.ds(h, 1), :]
-        mixed[:, cols(h)] = row.astype(jnp.bfloat16)
-        store(h).start()
+        out_ref[:, cols(h)] = row.astype(jnp.bfloat16)
 
     def diagonal(q, k):
         return jnp.where(causal, nt(k, q), LOW)
@@ -403,50 +399,6 @@
 
         each_head(drain)
 
-    def settle(h):
-        store(h).wait()
-
-    each_head(settle)
-
-
-def copy_kernel(chunks, src_ref, dst_ref, held, arrived, left):
-    rows = held.shape[0] // chunks
-    into = [
-        pltpu.make_async_copy(
-            src_ref.at[pl.ds(i * rows, rows)], held.at[pl.ds(i * rows, rows)], arrived.at[i]
-        )
-        for i in range(chunks)
-    ]
-    out = [
-        pltpu.make_async_copy(
-            held.at[pl.ds(i * rows, rows)], dst_ref.at[pl.ds(i * rows, rows)], left.at[i]
-        )
-        for i in range(chunks)
-    ]
-    for one in into:
-        one.start()
-    for one, other in zip(into, out):
-        one.wait()
-        other.start()
-    for other in out:
-        other.wait()
-
-
-def copied(array, chunks=4):
-    hbm = pl.BlockSpec(memory_space=pl.ANY)
-    return pl.pallas_call(
-        functools.partial(copy_kernel, chunks),
-        out_shape=jax.ShapeDtypeStruct(array.shape, array.dtype),
-        in_specs=[hbm],
-        out_specs=hbm,
-        scratch_shapes=[
-            pltpu.VMEM(array.shape, array.dtype),
-            pltpu.SemaphoreType.DMA((chunks,)),
-            pltpu.SemaphoreType.DMA((chunks,)),
-        ],
-        name="result_copy",
-    )(array)
-
 
 def hub_shards(n, queries, key_vectors, value_vectors, norm_gain, window_gain):
     tok, width = queries.shape
@@ -459,14 +411,14 @@
     state = pltpu.VMEM((heads, HEAD, HEAD), jnp.bfloat16)
     return pl.pallas_call(
         functools.partial(hub_kernel, n),
-        out_shape=jax.ShapeDtypeStruct((tok, width), jnp.bfloat16),
+        out_shape=pltpu.VMEM((tok, width), jnp.bfloat16),
         in_specs=[hbm] * 3 + [vmem] * 2,
-        out_specs=hbm,
+        out_specs=vmem,
         scratch_shapes=[block] * 4
         + [partial, partial, stats, state] * 2
-        + [block] * 4
+        + [block] * 3
         + [pltpu.SemaphoreType.DMA((8, heads)), pltpu.SemaphoreType.DMA((8, heads))]
-        + [pltpu.SemaphoreType.DMA((3,)), pltpu.SemaphoreType.DMA((heads,))],
+        + [pltpu.SemaphoreType.DMA((3,))],
         compiler_params=pltpu.CompilerParams(
             collective_id=0, has_side_effects=True, vmem_limit_bytes=56 * 2**20
         ),
@@ -487,7 +439,7 @@
         args = (queries, key_vectors, value_vectors, norm_gain, window_gain)
         fits = count * queries.shape[0] <= WINDOW
         if fits and count - 2 == 2:
-            return copied(hub_shards(count, *args))
+            return hub_shards(count, *args)
         return shards(*args)
 
     return jax.shard_map(

time: 72.7 us -> 71.1 us (0.978)
  Pallas kernels: 72.5 us -> 69.8 us
  local copies, waits for them, and re-layouts: 0 us -> 0.97 us
    pallas_call x2 -> x1, Pallas kernels: 72.5 us -> 69.8 us  [hub_shards(): pl.pallas_call(functools.partial(hub_kernel, n), out_shape=pltpu.VMEM((to...]
    unnamed x0 -> x1, local copies, waits for them, and re-layouts: none -> 0.97 us
where the time goes in v4:
time: 71.1 us; the launch traced here: 70.8 us
  Pallas kernels  69.8 us (98%)
  local copies, waits for them, and re-layouts  0.97 us (1%)
    pallas_call x1, Pallas kernels, hub_shards(): pl.pallas_call(functools.partial(hub_kernel, n), out_shape=pltpu.VMEM((to...  69.8 us

profile of v4, /device:TPU:30, one launch (start us, length us, event | category | flops | bytes accessed | tf_op | source)
XLA Modules:
  0.0 70.8 jit_solution(14473371554291420620)
XLA Ops:
  0.0 69.8 %hub_attention.1 = bf16[256,2048]{1,0:T(8,128)(2,1)S(1)} custom-call(bf16[256,2048]{1,0:T(8,128)(2,1)} %q_ref.1, bf16[256,2048]{1,0:T(8,128)(2,1)} %k_ref.1, bf16[256,2048]{1,0:T(8,128)(2,1)} %v_ref.1, f32[16,128]{1,0:T(8,128)} %bitcast.2, f32[16,128]{1,0:T(8,128)} %bitcast.3), custom_call_target="tpu_custom_call" | custom-call | tf_op jit(solution)/shard_map/hub_attention/pallas_call | solution.py:412
  69.8 1.0 %copy.7 = bf16[256,2048]{1,0:T(8,128)(2,1)} copy(bf16[256,2048]{1,0:T(8,128)(2,1)S(1)} %hub_attention.1) | data formatting | bytes 2097152

commit v5 on v4

--- a/solution.py
+++ b/solution.py
@@ -328,10 +328,16 @@
 
     @pl.when((me > hub) & (me < last))
     def _():
+        q_left(0).start()
+        q_left(1).start()
+
         def relay(h):
-            q_left(h).start()
             q_left(h).wait_recv()
             q_relay(h).start()
+
+            @pl.when((h > 0) & (h < heads - 1))
+            def _():
+                q_left(h + 1).start()
 
         each_head(relay)
 

time: 71.1 us -> 71.4 us (level)
  no operation moved by 1% of the time
where the time goes in v5:
time: 71.4 us; the launch traced here: 71.1 us
  Pallas kernels  70.2 us (98%)
  local copies, waits for them, and re-layouts  0.97 us (1%)
    pallas_call x1, Pallas kernels, hub_shards(): pl.pallas_call(functools.partial(hub_kernel, n), out_shape=pltpu.VMEM((to...  70.2 us

profile of v5, /device:TPU:30, one launch (start us, length us, event | category | flops | bytes accessed | tf_op | source)
XLA Modules:
  0.0 71.1 jit_solution(3241634184680907728)
XLA Ops:
  0.0 70.2 %hub_attention.1 = bf16[256,2048]{1,0:T(8,128)(2,1)S(1)} custom-call(bf16[256,2048]{1,0:T(8,128)(2,1)} %q_ref.1, bf16[256,2048]{1,0:T(8,128)(2,1)} %k_ref.1, bf16[256,2048]{1,0:T(8,128)(2,1)} %v_ref.1, f32[16,128]{1,0:T(8,128)} %bitcast.2, f32[16,128]{1,0:T(8,128)} %bitcast.3), custom_call_target="tpu_custom_call" | custom-call | tf_op jit(solution)/shard_map/hub_attention/pallas_call | solution.py:418
  70.2 1.0 %copy.7 = bf16[256,2048]{1,0:T(8,128)(2,1)} copy(bf16[256,2048]{1,0:T(8,128)(2,1)S(1)} %hub_attention.1) | data formatting | bytes 2097152
